TPU v7x, 128 devices: a whole 4x4x4 slice. The times are simulated.
128 devices in a mesh: seq: 128 (over x, y, z, core).
Axes of the slice: x: 4, y: 4, z: 4, core: 2. Of those that a mesh axis runs over, the one named last changes fastest.
Arguments:
- inputs: bfloat16 [131072, 768], P('seq'), may hold values from -6 to 6
- weight_one: bfloat16 [768, 3, 768], P('seq'), may hold values from -0.125 to 0.125
- weight_two: bfloat16 [768, 3, 768], P('seq'), may hold values from -0.125 to 0.125
- cotangent: bfloat16 [131072, 768], P('seq'), may hold values from -6 to 6
Outputs:
- outputs: bfloat16 [131072, 768], P('seq')
- input_grad: bfloat16 [131072, 768], P('seq')
- grad_one: float32 [768, 3, 768], P('seq')
- grad_two: float32 [768, 3, 768], P('seq')
All inputs are finite; a program needn't handle non-finite values.
Results may differ from a plain program's by a relative error of at most 0.0056.
Values may be sent and summed in bfloat16 or wider, within the bound.
A program may use at most 128 MiB of HBM per device.

v0:
```python
import math
import jax
import jax.numpy as jnp
from jax import lax
from jax.sharding import PartitionSpec as P

DILATION_A = 32
DILATION_B = 64


def padded_2(block, sides, width):
    for axis, dim in sides:
        count = lax.axis_size(axis)
        forward = [(i, i + 1) for i in range(count - 1)]
        backward = [(target, source) for source, target in forward]
        low = lax.ppermute(
            lax.slice_in_dim(block, block.shape[dim] - width, None, axis=dim), axis, forward
        )
        high = lax.ppermute(lax.slice_in_dim(block, 0, width, axis=dim), axis, backward)
        block = jnp.concatenate([low, block, high], axis=dim)
    return block


def normalize(layer_in):
    residual_in = layer_in.astype(jnp.float32)
    inv_rms = lax.rsqrt(jnp.mean(residual_in * residual_in, axis=-1, keepdims=True) + 1e-06)
    normed = residual_in * inv_rms
    active = (0.5 * normed * (1.0 + jax.scipy.special.erf(normed * 0.7071067811865476))).astype(
        jnp.bfloat16
    )
    return (residual_in, normed, inv_rms, active)


def slope_of(normed):
    return (
        0.5 * (1.0 + jax.scipy.special.erf(normed * 0.7071067811865476))
        + normed * jnp.exp(-0.5 * normed * normed) * 0.3989422804014327
    )


def fetch_forward(shard):
    return lax.all_gather(shard, "seq", axis=0, tiled=True)


def fetch_backward(shard):
    return lax.all_gather(shard, "seq", axis=0, tiled=True)


def forward_layer(layer_in, weight, spacing):
    residual_in, normed, inv_rms, active = normalize(layer_in)
    padded = padded_2(active, (("seq", 0),), spacing)
    length = layer_in.shape[0]
    mixed = jnp.zeros((length, weight.shape[2]), jnp.float32)
    for tap in range(3):
        mixed = mixed + jnp.dot(
            padded[tap * spacing : tap * spacing + length],
            weight[:, tap, :],
            preferred_element_type=jnp.float32,
        )
    return ((residual_in + mixed).astype(jnp.bfloat16), padded, normed, inv_rms)


def weight_term(padded, grad_out, spacing, grad_scale):
    length = grad_out.shape[0]
    terms = []
    for tap in range(3):
        window = padded[tap * spacing : tap * spacing + length]
        terms.append(
            lax.dot_general(
                window, grad_out, (((0,), (0,)), ((), ())), preferred_element_type=jnp.float32
            )
        )
    return jnp.stack(terms, axis=1) * grad_scale


def reduce_layer(padded, grad_out, spacing, grad_scale):
    whole_term = weight_term(padded, grad_out, spacing, grad_scale)
    return lax.psum_scatter(whole_term, "seq", scatter_dimension=0, tiled=True)


def backward_layer(grad_out, normed, inv_rms, weight, spacing):
    length = grad_out.shape[0]
    grad_pad = padded_2(grad_out, (("seq", 0),), spacing)
    act_grad = jnp.zeros((length, weight.shape[0]), jnp.float32)
    for tap in range(3):
        start_row = (2 - tap) * spacing
        act_grad = act_grad + lax.dot_general(
            grad_pad[start_row : start_row + length],
            weight[:, tap, :],
            (((1,), (1,)), ((), ())),
            preferred_element_type=jnp.float32,
        )
    norm_grad = act_grad * slope_of(normed)
    passed = grad_out.astype(jnp.float32) + inv_rms * (
        norm_grad - normed * jnp.mean(norm_grad * normed, axis=-1, keepdims=True)
    )
    return passed.astype(jnp.bfloat16)


def per_device(inputs, weight_one, weight_two, cotangent):
    grad_scale = 1.0 / math.sqrt(inputs.shape[0] * lax.axis_size("seq"))
    full_one = fetch_forward(weight_one)
    hidden, pad_one, normed_one, inv_one = forward_layer(inputs, full_one, DILATION_A)
    full_two = fetch_forward(weight_two)
    outputs, pad_two, normed_two, inv_two = forward_layer(hidden, full_two, DILATION_B)
    back_two = fetch_backward(weight_two)
    hidden_grad = backward_layer(cotangent, normed_two, inv_two, back_two, DILATION_B)
    grad_two = reduce_layer(pad_two, cotangent, DILATION_B, grad_scale)
    back_one = fetch_backward(weight_one)
    input_grad = backward_layer(hidden_grad, normed_one, inv_one, back_one, DILATION_A)
    grad_one = reduce_layer(pad_one, hidden_grad, DILATION_A, grad_scale)
    return (outputs, input_grad, grad_one, grad_two)


def solution(mesh):
    in_specs = (P("seq", None), P("seq", None, None), P("seq", None, None), P("seq", None))
    out_specs = (P("seq", None), P("seq", None), P("seq", None, None), P("seq", None, None))
    return jax.shard_map(
        per_device, mesh=mesh, in_specs=in_specs, out_specs=out_specs, check_vma=False
    )
```

profile of v0, /device:TPU:1, one launch (start us, length us, event | category | flops | bytes accessed | tf_op | source)
XLA Modules:
  0.0 380.1 jit_solution(17278720018428972216)
XLA Ops:
  8.7 1.9 fusion.22
  13.0 3.3 collective-permute-start.1
  16.4 3.5 collective-permute-start
  19.9 2.4 collective-permute-start.5
  22.3 1.9 collective-permute-start.4
  24.3 57.8 %all-gather.3.cloned.1.call-done = bf16[768,3,768]{2,1,0:T(4,128)(2,1)} async-done(((bf16[6,3,768]{2,1,0:T(4,128)(2,1)}), bf16[768,3,768]{2,1,0:T(4,128)(2,1)}) %all-gather.3.cloned.1.call-update) | async-done | bytes 3538960 | tf_op jit(solution)/shard_map/all_gather | solution.py:42
  82.0 12.4 %fusion.69 = (bf16[768,1,768]{2,1,0:T(2,128)(2,1)}, bf16[768,1,768]{2,1,0:T(2,128)(2,1)S(1)}, bf16[768,1,768]{2,1,0:T(2,128)(2,1)}) fusion(bf16[768,3,768]{2,1,0:T(4,128)(2,1)} %all-gather.3.cloned.1.call-done), kind=kLoop, calls=%fused_computation.105 | loop fusion | bytes 7077888 | tf_op jit(solution)/shard_map/slice | solution.py:57
  95.8 3.1 fusion.53
  98.9 50.7 %all-gather.5.cloned.1.call-done = bf16[768,3,768]{2,1,0:T(4,128)(2,1)} async-done(((bf16[6,3,768]{2,1,0:T(4,128)(2,1)}), bf16[768,3,768]{2,1,0:T(4,128)(2,1)}) %all-gather.5.cloned.1.call-update) | async-done | bytes 3538960 | tf_op jit(solution)/shard_map/all_gather | solution.py:42
  149.6 11.4 %fusion.68 = (bf16[768,1,768]{2,1,0:T(2,128)(2,1)S(1)}, bf16[768,1,768]{2,1,0:T(2,128)(2,1)S(1)}, bf16[768,1,768]{2,1,0:T(2,128)(2,1)S(1)}) fusion(bf16[768,3,768]{2,1,0:T(4,128)(2,1)} %all-gather.5.cloned.1.call-done), kind=kLoop, calls=%fused_computation.104 | loop fusion | bytes 7077888 | tf_op jit(solution)/shard_map/slice | solution.py:57
  162.5 1.9 copy-done.11
  165.6 2.2 fusion.48
  167.8 2.5 fusion.46
  170.5 2.6 fusion.36
  173.1 2.6 fusion.35
  175.8 2.1 fusion.31
  179.4 1.9 collective-permute-start.2
  181.4 2.4 collective-permute-start.3
  183.8 1.5 convolution_bitcast_fusion.4
  185.3 2.3 convolution_bitcast_fusion.3
  187.5 2.3 convolution_bitcast_fusion.5
  189.8 3.3 maximum_multiply_fusion
  193.1 1.5 convolution_bitcast_fusion
  194.6 1.5 convolution_bitcast_fusion.2
  196.1 3.2 maximum_multiply_fusion.1
  200.2 2.2 collective-permute-start.6
  202.4 3.1 fusion.55
  206.9 4.1 %collective-permute-start.7 = (bf16[32,768]{1,0:T(8,128)(2,1)S(1)}, bf16[32,768]{1,0:T(8,128)(2,1)S(1)}, u32[]{:S(2)}, u32[]{:S(2)}) collective-permute-start(bf16[32,768]{1,0:T(8,128)(2,1)S(1)} %get-tuple-element.26), channel_id=1, source_target_pairs={{0,1},{1,2},{2,3},{3,4},{4,5},{5,6},{6,7},{7,8},{8,9},{9,10},{10,1... | collective-permute-start | bytes 147464 | tf_op jit(solution)/shard_map/ppermute | solution.py:16
  212.5 2.6 fusion.21
  215.2 2.0 fusion.17
  219.5 2.8 fusion.37
  222.3 148.9 %all-reduce.5.cloned.1.call-done = (f32[768,3,768]{2,0,1:T(8,128)}, f32[768,3,768]{2,0,1:T(8,128)}) async-done(((f32[768,3,768]{2,0,1:T(8,128)}, f32[768,3,768]{2,0,1:T(8,128)}), (f32[768,3,768]{2,0,1:T(8,128)}, f32[768,3,768]{2,0,1:T(8,128)})) %all-reduce.5.cloned.1.call-update) | async-done | bytes 14155792
  (74 shorter events, 17.9 us)
Async XLA Ops:
  7.2 3.5 copy-start
  7.2 74.8 %all-gather.3.cloned.1.call-start = ((), (), s32[]{:S(2)}) async-start(), calls=%async_computation | async-start | bytes 4755456 | tf_op jit(solution)/shard_map/all_gather | solution.py:42
  7.9 141.7 %all-gather.5.cloned.1.call-start = ((), (), s32[]{:S(2)}) async-start(), calls=%async_computation.1 | async-start | bytes 4755456 | tf_op jit(solution)/shard_map/all_gather | solution.py:42
  8.7 11.2 %copy-start.16 = (bf16[1024,768]{1,0:T(8,128)(2,1)S(1)}, bf16[1024,768]{1,0:T(8,128)(2,1)}, u32[]{:S(2)}) copy-start(bf16[1024,768]{1,0:T(8,128)(2,1)} %param.7) | copy-start | bytes 4718596
  8.7 362.6 %all-reduce.5.cloned.1.call-start = ((), (), s32[]{:S(2)}) async-start(), calls=%async_computation.2 | async-start | bytes 28311552
  13.0 157.3 %collective-permute-start.1 = (bf16[32,768]{1,0:T(8,128)(2,1)S(1)}, bf16[32,768]{1,0:T(8,128)(2,1)}, u32[]{:S(2)}, u32[]{:S(2)}) collective-permute-start(bf16[32,768]{1,0:T(8,128)(2,1)S(1)} %get-tuple-element.32), channel_id=1, source_target_pairs={{1,0},{2,1},{3,2},{4,3},{5,4},{6,5},{7,6},{8,7},{9,8},{10,9},{11,1... | collective-permute-start | bytes 147464 | tf_op jit(solution)/shard_map/ppermute | solution.py:19
  16.4 146.1 %collective-permute-start = (bf16[32,768]{1,0:T(8,128)(2,1)S(1)}, bf16[32,768]{1,0:T(8,128)(2,1)}, u32[]{:S(2)}, u32[]{:S(2)}) collective-permute-start(bf16[32,768]{1,0:T(8,128)(2,1)S(1)} %get-tuple-element.33), channel_id=1, source_target_pairs={{0,1},{1,2},{2,3},{3,4},{4,5},{5,6},{6,7},{7,8},{8,9},{9,10},{10,1... | collective-permute-start | bytes 147464 | tf_op jit(solution)/shard_map/ppermute | solution.py:16
  19.9 153.2 %collective-permute-start.5 = (bf16[64,768]{1,0:T(8,128)(2,1)S(1)}, bf16[64,768]{1,0:T(8,128)(2,1)S(1)}, u32[]{:S(2)}, u32[]{:S(2)}) collective-permute-start(bf16[64,768]{1,0:T(8,128)(2,1)S(1)} %get-tuple-element.28), channel_id=1, source_target_pairs={{0,1},{1,2},{2,3},{3,4},{4,5},{5,6},{6,7},{7,8},{8,9},{9,10},{10,1... | collective-permute-start | bytes 294920 | tf_op jit(solution)/shard_map/ppermute | solution.py:16
  22.3 145.5 %collective-permute-start.4 = (bf16[64,768]{1,0:T(8,128)(2,1)S(1)}, bf16[64,768]{1,0:T(8,128)(2,1)}, u32[]{:S(2)}, u32[]{:S(2)}) collective-permute-start(bf16[64,768]{1,0:T(8,128)(2,1)S(1)} %get-tuple-element.29), channel_id=1, source_target_pairs={{1,0},{2,1},{3,2},{4,3},{5,4},{6,5},{7,6},{8,7},{9,8},{10,9},{11,1... | collective-permute-start | bytes 294920 | tf_op jit(solution)/shard_map/ppermute | solution.py:19
  82.0 13.8 %copy-start.19 = (bf16[1024,768]{1,0:T(8,128)(2,1)S(1)}, bf16[1024,768]{1,0:T(8,128)(2,1)}, u32[]{:S(2)}) copy-start(bf16[1024,768]{1,0:T(8,128)(2,1)} %copy-done.18) | copy-start | bytes 4718596
  94.4 1.4 copy-start.13
  161.0 1.5 copy-start.15
  161.0 6.8 %copy-start.7 = (bf16[768,1,768]{2,1,0:T(2,128)(2,1)}, bf16[768,1,768]{2,1,0:T(2,128)(2,1)S(1)}, u32[]{:S(2)}) copy-start(bf16[768,1,768]{2,1,0:T(2,128)(2,1)S(1)} %get-tuple-element.20) | copy-start | bytes 3538948
  161.0 12.1 %copy-start.5 = (bf16[768,1,768]{2,1,0:T(2,128)(2,1)}, bf16[768,1,768]{2,1,0:T(2,128)(2,1)S(1)}, u32[]{:S(2)}) copy-start(bf16[768,1,768]{2,1,0:T(2,128)(2,1)S(1)} %get-tuple-element.18) | copy-start | bytes 3538948
  161.0 3.4 copy-start.11
  161.0 4.6 %copy-start.20 = (bf16[1024,768]{1,0:T(8,128)(2,1)S(1)}, bf16[1024,768]{1,0:T(8,128)(2,1)}, u32[]{:S(2)}) copy-start(bf16[1024,768]{1,0:T(8,128)(2,1)} %copy-done.18) | copy-start | bytes 4718596
  167.8 2.5 copy-start.9
  167.8 2.6 copy-start.21
  173.1 2.7 copy-start.3
  173.1 2.7 copy-start.17
  177.9 9.6 %copy-start.1 = (bf16[1024,768]{1,0:T(8,128)(2,1)}, bf16[1024,768]{1,0:T(8,128)(2,1)S(1)}, u32[]{:S(2)}) copy-start(bf16[1024,768]{1,0:T(8,128)(2,1)S(1)} %get-tuple-element.24) | copy-start | bytes 4718596
  179.4 15.1 %collective-permute-start.2 = (bf16[64,768]{1,0:T(8,128)(2,1)S(1)}, bf16[64,768]{1,0:T(8,128)(2,1)S(1)}, u32[]{:S(2)}, u32[]{:S(2)}) collective-permute-start(bf16[64,768]{1,0:T(8,128)(2,1)S(1)} %get-tuple-element.31), channel_id=1, source_target_pairs={{0,1},{1,2},{2,3},{3,4},{4,5},{5,6},{6,7},{7,8},{8,9},{9,10},{10,1... | collective-permute-start | bytes 294920 | tf_op jit(solution)/shard_map/ppermute | solution.py:16
  181.4 11.7 %collective-permute-start.3 = (bf16[64,768]{1,0:T(8,128)(2,1)S(1)}, bf16[64,768]{1,0:T(8,128)(2,1)S(1)}, u32[]{:S(2)}, u32[]{:S(2)}) collective-permute-start(bf16[64,768]{1,0:T(8,128)(2,1)S(1)} %get-tuple-element.30), channel_id=1, source_target_pairs={{1,0},{2,1},{3,2},{4,3},{5,4},{6,5},{7,6},{8,7},{9,8},{10,9},{11,1... | collective-permute-start | bytes 294920 | tf_op jit(solution)/shard_map/ppermute | solution.py:19
  200.2 5.3 %copy-start.2 = (bf16[1024,768]{1,0:T(8,128)(2,1)S(1)}, bf16[1024,768]{1,0:T(8,128)(2,1)}, u32[]{:S(2)}) copy-start(bf16[1024,768]{1,0:T(8,128)(2,1)} %copy-done.1) | copy-start | bytes 4718596
  200.2 5.3 %copy-start.14 = (bf16[768,1,768]{2,1,0:T(2,128)(2,1)S(1)}, bf16[768,1,768]{2,1,0:T(2,128)(2,1)}, u32[]{:S(2)}) copy-start(bf16[768,1,768]{2,1,0:T(2,128)(2,1)} %copy-done.13) | copy-start | bytes 3538948
  200.2 10.9 %collective-permute-start.6 = (bf16[32,768]{1,0:T(8,128)(2,1)S(1)}, bf16[32,768]{1,0:T(8,128)(2,1)S(1)}, u32[]{:S(2)}, u32[]{:S(2)}) collective-permute-start(bf16[32,768]{1,0:T(8,128)(2,1)S(1)} %get-tuple-element.27), channel_id=1, source_target_pairs={{1,0},{2,1},{3,2},{4,3},{5,4},{6,5},{7,6},{8,7},{9,8},{10,9},{11,1... | collective-permute-start | bytes 147464 | tf_op jit(solution)/shard_map/ppermute | solution.py:19
  205.4 5.6 %copy-start.12 = (bf16[768,1,768]{2,1,0:T(2,128)(2,1)S(1)}, bf16[768,1,768]{2,1,0:T(2,128)(2,1)}, u32[]{:S(2)}) copy-start(bf16[768,1,768]{2,1,0:T(2,128)(2,1)} %get-tuple-element.23) | copy-start | bytes 3538948
  206.9 5.6 %copy-start.10 = (bf16[768,1,768]{2,1,0:T(2,128)(2,1)S(1)}, bf16[768,1,768]{2,1,0:T(2,128)(2,1)}, u32[]{:S(2)}) copy-start(bf16[768,1,768]{2,1,0:T(2,128)(2,1)} %get-tuple-element.21) | copy-start | bytes 3538948
  206.9 5.6 %collective-permute-start.7 = (bf16[32,768]{1,0:T(8,128)(2,1)S(1)}, bf16[32,768]{1,0:T(8,128)(2,1)S(1)}, u32[]{:S(2)}, u32[]{:S(2)}) collective-permute-start(bf16[32,768]{1,0:T(8,128)(2,1)S(1)} %get-tuple-element.26), channel_id=1, source_target_pairs={{0,1},{1,2},{2,3},{3,4},{4,5},{5,6},{6,7},{7,8},{8,9},{9,10},{10,1... | collective-permute-start | bytes 147464 | tf_op jit(solution)/shard_map/ppermute | solution.py:16
  215.2 2.0 copy-start.8
  217.2 1.5 copy-start.4
  217.2 2.3 copy-start.6
  (1 other events, 1.1 us)
Sparse Core Ops, SparseCore 0:
  11.0 70.9 all-gather.2
  85.0 64.5 all-gather.4
  199.4 171.7 all-reduce.4
where the time goes:
time: 381 us; the launch traced here: 380 us
  waiting for transfers between devices  259 us (68%)
  matrix products  37.6 us (10%)
  local copies, waits for them, and re-layouts  33.7 us (9%)
  starting transfers between devices  21.9 us (6%)
  between operations  14.3 us (4%)
  other arithmetic  13.8 us (4%)
    unnamed x4, waiting for transfers between devices  150 us
    all_gather x2, waiting for transfers between devices, fetch_forward(): return lax.all_gather(shard, 'seq', axis=0, tiled=True)  109 us
    slice x2, local copies, waits for them, and re-layouts, forward_layer(): weight[:, tap, :]  23.7 us
    dot_general x6, matrix products, forward_layer(): jnp.dot(padded[tap * spacing:tap * spacing + length], weight[:, tap, :],...  15.1 us
    dot_general x6, matrix products, backward_layer(): lax.dot_general(grad_pad[start_row:start_row + length], weight[:, tap, :]...  12 us
    ppermute x4, starting transfers between devices, padded_2(): lax.ppermute(lax.slice_in_dim(block, block.shape[dim] - width, None, axis...  12 us
    dot_general x6, matrix products, weight_term(): lax.dot_general(window, grad_out, (((0,), (0,)), ((), ())), preferred_ele...  10.4 us
    ppermute x4, starting transfers between devices, padded_2(): lax.ppermute(lax.slice_in_dim(block, 0, width, axis=dim), axis, backward)  9.84 us
  transfers between devices with their start and end apart: 11, of which 3 were waited for; matrix products, arithmetic and copies ran while one was open for 17% of the time, Pallas kernels for 0%

commit v1 on v0

--- a/solution.py
+++ b/solution.py
@@ -39,7 +39,9 @@
 
 
 def fetch_forward(shard):
-    return lax.all_gather(shard, "seq", axis=0, tiled=True)
+    return jnp.concatenate(
+        lax.all_to_all(jnp.stack([shard] * lax.axis_size("seq")), "seq", 0, 0), axis=0
+    )
 
 
 def fetch_backward(shard):

time: 381 us -> 427 us (1.12)
  local copies, waits for them, and re-layouts: 33.7 us -> 57.8 us
  starting transfers between devices: 21.9 us -> 38.9 us
    all_to_all x0 -> x2, waiting for transfers between devices: none -> 45.5 us  [fetch_forward(): lax.all_to_all(jnp.stack([shard] * lax.axis_size('seq')), 'seq', 0, 0)]
    all_gather x2, waiting for transfers between devices: 109 us -> 65.7 us  [fetch_backward(): return lax.all_gather(shard, 'seq', axis=0, tiled=True)]
    all_to_all x0 -> x2, starting transfers between devices: none -> 18.2 us  [fetch_forward(): lax.all_to_all(jnp.stack([shard] * lax.axis_size('seq')), 'seq', 0, 0)]
    reshape x0 -> x2, local copies, waits for them, and re-layouts: none -> 13.8 us  [fetch_forward(): jnp.concatenate(lax.all_to_all(jnp.stack([shard] * lax.axis_size('seq')),...]
    all_to_all x0 -> x2, local copies, waits for them, and re-layouts: none -> 9.71 us  [fetch_forward(): lax.all_to_all(jnp.stack([shard] * lax.axis_size('seq')), 'seq', 0, 0)]
    another operation x0 -> x2, local copies, waits for them, and re-layouts: none -> 4.99 us  [fetch_forward(): jnp.stack([shard] * lax.axis_size('seq'))]
    unnamed x47 -> x29, local copies, waits for them, and re-layouts: 9.1 us -> 5.05 us
  transfers between devices with their start and end apart: 11 -> 13, of which waited for: 3 -> 4; matrix products, arithmetic and copies ran while one was open for 17% -> 25% of each run, Pallas kernels for 0% -> 0%
where the time goes in v1:
time: 427 us; the launch traced here: 426 us
  waiting for transfers between devices  261 us (61%)
  local copies, waits for them, and re-layouts  57.8 us (14%)
  matrix products  40.6 us (10%)
  starting transfers between devices  38.9 us (9%)
  between operations  14.2 us (3%)
  other arithmetic  13.5 us (3%)
    unnamed x4, waiting for transfers between devices  149 us
    all_gather x2, waiting for transfers between devices, fetch_backward(): return lax.all_gather(shard, 'seq', axis=0, tiled=True)  65.7 us
    all_to_all x2, waiting for transfers between devices, fetch_forward(): lax.all_to_all(jnp.stack([shard] * lax.axis_size('seq')), 'seq', 0, 0)  45.5 us
    slice x2, local copies, waits for them, and re-layouts, backward_layer(): weight[:, tap, :]  22.5 us
    all_to_all x2, starting transfers between devices, fetch_forward(): lax.all_to_all(jnp.stack([shard] * lax.axis_size('seq')), 'seq', 0, 0)  18.2 us
    dot_general x6, matrix products, forward_layer(): jnp.dot(padded[tap * spacing:tap * spacing + length], weight[:, tap, :],...  16.9 us
    reshape x2, local copies, waits for them, and re-layouts, fetch_forward(): jnp.concatenate(lax.all_to_all(jnp.stack([shard] * lax.axis_size('seq')),...  13.8 us
    dot_general x6, matrix products, backward_layer(): lax.dot_general(grad_pad[start_row:start_row + length], weight[:, tap, :]...  13.4 us
  transfers between devices with their start and end apart: 13, of which 4 were waited for; matrix products, arithmetic and copies ran while one was open for 25% of the time, Pallas kernels for 0%

profile of v1, /device:TPU:1, one launch (start us, length us, event | category | flops | bytes accessed | tf_op | source)
XLA Modules:
  0.0 425.6 jit_solution(8928202690675994422)
XLA Ops:
  8.7 2.5 stack.20
  11.2 11.9 %all-to-all-start = ((bf16[128,6,3,768]{3,1,2,0:T(8,128)(2,1)}), bf16[128,6,3,768]{3,1,2,0:T(8,128)(2,1)}, u32[]{:S(2)}, u32[]{:S(2)}) async-start(bf16[128,6,3,768]{3,1,2,0:T(8,128)(2,1)} %stack.20), calls=%async_computation | async-start | bytes 9437184 | tf_op jit(solution)/shard_map/all_to_all | solution.py:43
  24.9 3.0 collective-permute-start.1
  27.9 2.5 collective-permute-start
  31.4 2.4 collective-permute-start.5
  33.8 2.5 collective-permute-start.4
  36.4 45.5 %all-to-all-done = bf16[128,6,3,768]{3,1,2,0:T(8,128)(2,1)} async-done(((bf16[128,6,3,768]{3,1,2,0:T(8,128)(2,1)}), bf16[128,6,3,768]{3,1,2,0:T(8,128)(2,1)}, u32[]{:S(2)}, u32[]{:S(2)}) %all-to-all-start) | async-done | bytes 3538976 | tf_op jit(solution)/shard_map/all_to_all | solution.py:43
  81.9 2.4 stack.21
  84.3 6.3 %all-to-all-start.1 = ((bf16[128,6,3,768]{3,1,2,0:T(8,128)(2,1)}), bf16[128,6,3,768]{3,1,2,0:T(8,128)(2,1)}, u32[]{:S(2)}, u32[]{:S(2)}) async-start(bf16[128,6,3,768]{3,1,2,0:T(8,128)(2,1)} %stack.21), calls=%async_computation.1 | async-start | bytes 9437184 | tf_op jit(solution)/shard_map/all_to_all | solution.py:43
  90.9 4.9 %copy.32 = bf16[128,6,3,768]{3,1,0,2:T(8,128)(2,1)} copy(bf16[128,6,3,768]{3,1,2,0:T(8,128)(2,1)} %all-to-all-done) | data formatting | bytes 7077888 | tf_op jit(solution)/shard_map/all_to_all | solution.py:43
  95.8 6.9 %reshape.42 = bf16[768,3,768]{2,0,1:T(8,128)(2,1)} reshape(bf16[128,6,3,768]{3,1,0,2:T(8,128)(2,1)} %copy.32) | data formatting | bytes 7077888 | tf_op jit(solution)/shard_map/reshape | solution.py:42
  102.7 2.8 fusion.52
  107.8 3.3 fusion.36
  111.1 63.7 %all-gather.3.cloned.1.call-done = bf16[768,3,768]{2,1,0:T(4,128)(2,1)} async-done(((bf16[6,3,768]{2,1,0:T(4,128)(2,1)}), bf16[768,3,768]{2,1,0:T(4,128)(2,1)}) %all-gather.3.cloned.1.call-update) | async-done | bytes 3538960 | tf_op jit(solution)/shard_map/all_gather | solution.py:48
  174.8 11.2 %fusion.69 = (bf16[768,1,768]{2,1,0:T(2,128)(2,1)S(1)}, bf16[768,1,768]{2,1,0:T(2,128)(2,1)S(1)}, bf16[768,1,768]{2,1,0:T(2,128)(2,1)S(1)}) fusion(bf16[768,3,768]{2,1,0:T(4,128)(2,1)} %all-gather.3.cloned.1.call-done), kind=kLoop, calls=%fused_computation.111 | loop fusion | bytes 7077888 | tf_op jit(solution)/shard_map/slice | solution.py:91
  187.5 2.3 fusion.46
  189.9 3.4 fusion.35
  193.3 3.4 fusion.31
  198.6 2.6 collective-permute-start.3
  201.3 2.3 convolution_bitcast_fusion.3
  205.0 2.3 convolution_bitcast_fusion.5
  208.8 3.3 maximum_multiply_fusion
  215.0 3.2 maximum_multiply_fusion.1
  218.2 4.8 %copy.34 = bf16[128,6,3,768]{3,1,0,2:T(8,128)(2,1)} copy(bf16[128,6,3,768]{3,1,2,0:T(8,128)(2,1)} %all-to-all-done.1) | data formatting | bytes 7077888 | tf_op jit(solution)/shard_map/all_to_all | solution.py:43
  223.0 7.0 %reshape.43 = bf16[768,3,768]{2,0,1:T(8,128)(2,1)} reshape(bf16[128,6,3,768]{3,1,0,2:T(8,128)(2,1)} %copy.34) | data formatting | bytes 7077888 | tf_op jit(solution)/shard_map/reshape | solution.py:42
  230.8 3.1 collective-permute-start.7
  236.1 4.3 %fusion.49 = f32[1024,768]{1,0:T(8,128)} fusion(bf16[1024,768]{1,0:T(8,128)(2,1)S(1)} %get-tuple-element.29, bf16[768,3,768]{2,0,1:T(8,128)(2,1)} %reshape.43), kind=kOutput, calls=%fused_computation.75 | convolution fusion | flops 1207959552 | bytes 5898240 | tf_op jit(solution)/shard_map/dot_general | solution.py:57
  242.4 11.2 %fusion.68 = (bf16[768,1,768]{2,1,0:T(2,128)(2,1)S(1)}, bf16[768,1,768]{2,1,0:T(2,128)(2,1)S(1)}, bf16[768,1,768]{2,1,0:T(2,128)(2,1)S(1)}) fusion(bf16[768,3,768]{2,1,0:T(4,128)(2,1)} %all-gather.5.cloned.1.call-done), kind=kLoop, calls=%fused_computation.110 | loop fusion | bytes 7077888 | tf_op jit(solution)/shard_map/slice | solution.py:91
  255.1 2.2 fusion.42
  257.4 2.6 fusion.21
  265.4 2.8 fusion.37
  268.1 148.6 %all-reduce.5.cloned.1.call-done = (f32[768,3,768]{2,0,1:T(8,128)}, f32[768,3,768]{2,0,1:T(8,128)}) async-done(((f32[768,3,768]{2,0,1:T(8,128)}, f32[768,3,768]{2,0,1:T(8,128)}), (f32[768,3,768]{2,0,1:T(8,128)}, f32[768,3,768]{2,0,1:T(8,128)})) %all-reduce.5.cloned.1.call-update) | async-done | bytes 14155792
  (66 shorter events, 29.9 us)
Async XLA Ops:
  7.2 167.7 %all-gather.3.cloned.1.call-start = ((), (), s32[]{:S(2)}) async-start(), calls=%async_computation.2 | async-start | bytes 4755456 | tf_op jit(solution)/shard_map/all_gather | solution.py:48
  11.2 12.0 %copy-start = (bf16[1024,768]{1,0:T(8,128)(2,1)S(1)}, bf16[1024,768]{1,0:T(8,128)(2,1)}, u32[]{:S(2)}) copy-start(bf16[1024,768]{1,0:T(8,128)(2,1)} %param.4) | copy-start | bytes 4718596
  11.2 70.7 %all-to-all-start = ((bf16[128,6,3,768]{3,1,2,0:T(8,128)(2,1)}), bf16[128,6,3,768]{3,1,2,0:T(8,128)(2,1)}, u32[]{:S(2)}, u32[]{:S(2)}) async-start(bf16[128,6,3,768]{3,1,2,0:T(8,128)(2,1)} %stack.20), calls=%async_computation | async-start | bytes 9437184 | tf_op jit(solution)/shard_map/all_to_all | solution.py:43
  23.1 13.3 %copy-start.11 = (bf16[6,3,768]{2,1,0:T(4,128)(2,1)S(1)}, bf16[6,3,768]{2,1,0:T(4,128)(2,1)}, u32[]{:S(2)}) copy-start(bf16[6,3,768]{2,1,0:T(4,128)(2,1)} %param.6) | copy-start | bytes 82948
  23.1 219.3 %all-gather.5.cloned.1.call-start = ((), (), s32[]{:S(2)}) async-start(), calls=%async_computation.3 | async-start | bytes 4755456 | tf_op jit(solution)/shard_map/all_gather | solution.py:48
  24.8 80.7 %copy-start.9 = (bf16[1024,768]{1,0:T(8,128)(2,1)}, bf16[1024,768]{1,0:T(8,128)(2,1)S(1)}, u32[]{:S(2)}) copy-start(bf16[1024,768]{1,0:T(8,128)(2,1)S(1)} %fusion.11) | copy-start | bytes 4718596
  24.9 82.9 %collective-permute-start.1 = (bf16[32,768]{1,0:T(8,128)(2,1)S(1)}, bf16[32,768]{1,0:T(8,128)(2,1)}, u32[]{:S(2)}, u32[]{:S(2)}) collective-permute-start(bf16[32,768]{1,0:T(8,128)(2,1)S(1)} %get-tuple-element.36), channel_id=1, source_target_pairs={{1,0},{2,1},{3,2},{4,3},{5,4},{6,5},{7,6},{8,7},{9,8},{10,9},{11,1... | collective-permute-start | bytes 147464 | tf_op jit(solution)/shard_map/ppermute | solution.py:19
  27.9 77.6 %collective-permute-start = (bf16[32,768]{1,0:T(8,128)(2,1)S(1)}, bf16[32,768]{1,0:T(8,128)(2,1)}, u32[]{:S(2)}, u32[]{:S(2)}) collective-permute-start(bf16[32,768]{1,0:T(8,128)(2,1)S(1)} %get-tuple-element.37), channel_id=1, source_target_pairs={{0,1},{1,2},{2,3},{3,4},{4,5},{5,6},{6,7},{7,8},{8,9},{9,10},{10,1... | collective-permute-start | bytes 147464 | tf_op jit(solution)/shard_map/ppermute | solution.py:16
  31.4 158.4 %collective-permute-start.5 = (bf16[64,768]{1,0:T(8,128)(2,1)S(1)}, bf16[64,768]{1,0:T(8,128)(2,1)}, u32[]{:S(2)}, u32[]{:S(2)}) collective-permute-start(bf16[64,768]{1,0:T(8,128)(2,1)S(1)} %get-tuple-element.32), channel_id=1, source_target_pairs={{0,1},{1,2},{2,3},{3,4},{4,5},{5,6},{6,7},{7,8},{8,9},{9,10},{10,1... | collective-permute-start | bytes 294920 | tf_op jit(solution)/shard_map/ppermute | solution.py:16
  33.8 153.7 %collective-permute-start.4 = (bf16[64,768]{1,0:T(8,128)(2,1)S(1)}, bf16[64,768]{1,0:T(8,128)(2,1)}, u32[]{:S(2)}, u32[]{:S(2)}) collective-permute-start(bf16[64,768]{1,0:T(8,128)(2,1)S(1)} %get-tuple-element.33), channel_id=1, source_target_pairs={{1,0},{2,1},{3,2},{4,3},{5,4},{6,5},{7,6},{8,7},{9,8},{10,9},{11,1... | collective-permute-start | bytes 294920 | tf_op jit(solution)/shard_map/ppermute | solution.py:19
  84.3 133.9 %all-to-all-start.1 = ((bf16[128,6,3,768]{3,1,2,0:T(8,128)(2,1)}), bf16[128,6,3,768]{3,1,2,0:T(8,128)(2,1)}, u32[]{:S(2)}, u32[]{:S(2)}) async-start(bf16[128,6,3,768]{3,1,2,0:T(8,128)(2,1)} %stack.21), calls=%async_computation.1 | async-start | bytes 9437184 | tf_op jit(solution)/shard_map/all_to_all | solution.py:43
  90.7 326.1 %all-reduce.5.cloned.1.call-start = ((), (), s32[]{:S(2)}) async-start(), calls=%async_computation.4 | async-start | bytes 28311552
  102.7 2.9 copy-start.6
  111.1 78.7 %copy-start.4 = (bf16[1024,768]{1,0:T(8,128)(2,1)}, bf16[1024,768]{1,0:T(8,128)(2,1)S(1)}, u32[]{:S(2)}) copy-start(bf16[1024,768]{1,0:T(8,128)(2,1)S(1)} %get-tuple-element.39) | copy-start | bytes 4718596
  174.8 11.2 %copy-start.8 = (bf16[1024,768]{1,0:T(8,128)(2,1)S(1)}, bf16[1024,768]{1,0:T(8,128)(2,1)}, u32[]{:S(2)}) copy-start(bf16[1024,768]{1,0:T(8,128)(2,1)} %param.7) | copy-start | bytes 4718596
  193.2 8.0 %copy-start.10 = (bf16[1024,768]{1,0:T(8,128)(2,1)S(1)}, bf16[1024,768]{1,0:T(8,128)(2,1)}, u32[]{:S(2)}) copy-start(bf16[1024,768]{1,0:T(8,128)(2,1)} %copy-done.9) | copy-start | bytes 4718596
  196.7 8.4 %copy-start.1 = (bf16[1024,768]{1,0:T(8,128)(2,1)}, bf16[1024,768]{1,0:T(8,128)(2,1)S(1)}, u32[]{:S(2)}) copy-start(bf16[1024,768]{1,0:T(8,128)(2,1)S(1)} %get-tuple-element.28) | copy-start | bytes 4718596
  196.7 16.8 %collective-permute-start.2 = (bf16[64,768]{1,0:T(8,128)(2,1)S(1)}, bf16[64,768]{1,0:T(8,128)(2,1)S(1)}, u32[]{:S(2)}, u32[]{:S(2)}) collective-permute-start(bf16[64,768]{1,0:T(8,128)(2,1)S(1)} %get-tuple-element.35), channel_id=1, source_target_pairs={{0,1},{1,2},{2,3},{3,4},{4,5},{5,6},{6,7},{7,8},{8,9},{9,10},{10,1... | collective-permute-start | bytes 294920 | tf_op jit(solution)/shard_map/ppermute | solution.py:16
  198.6 13.4 %collective-permute-start.3 = (bf16[64,768]{1,0:T(8,128)(2,1)S(1)}, bf16[64,768]{1,0:T(8,128)(2,1)S(1)}, u32[]{:S(2)}, u32[]{:S(2)}) collective-permute-start(bf16[64,768]{1,0:T(8,128)(2,1)S(1)} %get-tuple-element.34), channel_id=1, source_target_pairs={{1,0},{2,1},{3,2},{4,3},{5,4},{6,5},{7,6},{8,7},{9,8},{10,9},{11,1... | collective-permute-start | bytes 294920 | tf_op jit(solution)/shard_map/ppermute | solution.py:19
  230.8 26.6 %collective-permute-start.7 = (bf16[32,768]{1,0:T(8,128)(2,1)S(1)}, bf16[32,768]{1,0:T(8,128)(2,1)S(1)}, u32[]{:S(2)}, u32[]{:S(2)}) collective-permute-start(bf16[32,768]{1,0:T(8,128)(2,1)S(1)} %get-tuple-element.30), channel_id=1, source_target_pairs={{0,1},{1,2},{2,3},{3,4},{4,5},{5,6},{6,7},{7,8},{8,9},{9,10},{10,1... | collective-permute-start | bytes 147464 | tf_op jit(solution)/shard_map/ppermute | solution.py:16
  233.9 21.2 %collective-permute-start.6 = (bf16[32,768]{1,0:T(8,128)(2,1)S(1)}, bf16[32,768]{1,0:T(8,128)(2,1)}, u32[]{:S(2)}, u32[]{:S(2)}) collective-permute-start(bf16[32,768]{1,0:T(8,128)(2,1)S(1)} %get-tuple-element.31), channel_id=1, source_target_pairs={{1,0},{2,1},{3,2},{4,3},{5,4},{6,5},{7,6},{8,7},{9,8},{10,9},{11,1... | collective-permute-start | bytes 147464 | tf_op jit(solution)/shard_map/ppermute | solution.py:19
  242.4 11.3 %copy-start.2 = (bf16[1024,768]{1,0:T(8,128)(2,1)S(1)}, bf16[1024,768]{1,0:T(8,128)(2,1)}, u32[]{:S(2)}) copy-start(bf16[1024,768]{1,0:T(8,128)(2,1)} %copy-done.1) | copy-start | bytes 4718596
  260.0 2.7 copy-start.3
  262.8 1.5 copy-start.5
  262.8 2.6 copy-start.7
Sparse Core Ops, SparseCore 0:
  11.0 163.7 all-gather.2
  177.9 64.5 all-gather.4
  247.6 169.1 all-reduce.4
